TPU v7x, 256 devices: a whole 4x4x8 slice. The times are simulated.
256 devices in a mesh: seq: 32 (over y, z), head: 8 (over x, core).
Axes of the slice: x: 4, y: 4, z: 8, core: 2. Of those that a mesh axis runs over, the one named last changes fastest.
Arguments:
- hidden: bfloat16 [16384, 8192], P('seq', 'head'), may hold values from -6 to 6
- gain: float32 [8192], replicated, may hold values from 0.25 to 1.75
- key_matrix: bfloat16 [8192, 1024], P(None, 'head'), may hold values from -0.0625 to 0.0625
- value_matrix: bfloat16 [8192, 1024], P(None, 'head'), may hold values from -0.0625 to 0.0625
- queries: bfloat16 [64, 8192], P(None, 'head'), may hold values from -360 to 360
- window_len: int32 [8], P('head'), may hold values from 16 to 64, as said below
- kernel_width: int32 [8], P('head'), may hold values from 1 to 15, as said below
- kept_block_count: int32 [8], P('head'), may hold values from 1 to 64
Outputs:
- block_scores: float32 [8, 128], P('head', 'seq')
- kept_fraction: float32 [8], P('head')
Inputs may be any that keep to these rules, and one draw needn't show every extreme that they name: `window_len`: at least one key-value head uses all 64 window queries. `kernel_width`: odd; at least one key-value head has width 15.
All inputs are finite; a program needn't handle non-finite values.
Results may differ from a plain program's by a relative error of at most 0.0112.
The roundings to bfloat16 on the way count: a program that leaves them out, or rounds other values in their place, can miss the bound.
Values may be sent and summed in bfloat16 or wider, within the bound.
A program may use at most 128 MiB of HBM per device.

v0:
```python
import jax
import jax.numpy as jnp
from jax import lax
from jax.sharding import PartitionSpec as P

BLK = 128
KERNEL_LIMIT = 15


def copy_for_each(x, axis):
    count = lax.axis_size(axis)
    return lax.all_to_all(jnp.broadcast_to(x[None], (count, *x.shape)), axis, 0, 0, tiled=True)


def taken_together(x, axis):
    return copy_for_each(x, axis).sum(axis=0)


def gathered_once(x, axis):
    leaves = jax.tree.leaves(x)
    order = sorted(range(len(leaves)), key=lambda k: -leaves[k].size)
    width = (1, *leaves[order[0]].shape)[-1]
    lines = [
        jnp.pad(leaves[k].reshape(-1), (0, -leaves[k].size % width)).reshape(-1, width)
        for k in order
    ]
    both, at, found = (copy_for_each(jnp.concatenate(lines), axis), 0, {})
    for k, line in zip(order, lines):
        section = both[:, at : at + len(line)].reshape(len(both), -1)
        found[k] = section[:, : leaves[k].size].reshape(-1, *leaves[k].shape)
        at += len(line)
    numbers = iter(range(len(leaves)))
    return jax.tree.map(lambda _: found[next(numbers)], x)


def combined_pairwise(pieces, combine):
    while len(jax.tree.leaves(pieces)[0]) > 1:
        pieces = jax.vmap(combine)(
            *(jax.tree.map(lambda part: part[side::2], pieces) for side in (0, 1))
        )
    return jax.tree.map(lambda part: part[0], pieces)


def joined_all(x, axis, combine):
    pieces = gathered_once(x, axis)
    return combined_pairwise(pieces, combine)


def with_halo(x, sides, width):
    for axis, dim in sides:
        count, length = (lax.axis_size(axis), x.shape[dim])
        up = [(i, (i + 1) % count) for i in range(count - 1)]
        down = [(j, i) for i, j in up]
        last = lax.slice_in_dim(x, length - width, length, axis=dim)
        leading = lax.slice_in_dim(x, 0, width, axis=dim)
        before = lax.ppermute(last, axis, up)
        after = lax.ppermute(leading, axis, down)
        x = jnp.concatenate([before, x, after], axis=dim)
    return x


def laid_out(tiles, dim):
    lengths = list(tiles.shape[1:])
    lengths[dim] *= tiles.shape[0]
    return jnp.moveaxis(tiles, 0, dim).reshape(lengths)


def gathered_copies(x, axis, dim):
    return laid_out(copy_for_each(x, axis), dim)


def rotate(raw, positions):
    half = raw.shape[1] // 2
    freq = 500000.0 ** (-(jnp.arange(half).astype(jnp.float32) * 2.0) / raw.shape[1])
    angle = positions[:, None] * freq[None, :]
    leading_part = raw[:, :half]
    trailing_part = raw[:, half:]
    return jnp.concatenate(
        [
            leading_part * jnp.cos(angle) - trailing_part * jnp.sin(angle),
            trailing_part * jnp.cos(angle) + leading_part * jnp.sin(angle),
        ],
        axis=1,
    )


def combine_stats(earlier, later):
    top = jnp.maximum(earlier[0], later[0])
    total = earlier[1] * jnp.exp(earlier[0] - top) + later[1] * jnp.exp(later[0] - top)
    return (top, total)


def local(
    hidden, gain, key_matrix, value_matrix, queries, window_len, kernel_width, kept_block_count
):
    tok_rows = hidden.shape[0]
    full_width = gain.shape[0]
    head_size = key_matrix.shape[1]
    floats = hidden.astype(jnp.float32)
    sumsq = taken_together(jnp.sum(floats * floats, axis=1), "head")
    inv_rms = lax.rsqrt(sumsq / full_width + 1e-05)
    joined = jnp.concatenate([key_matrix, value_matrix], axis=1)
    normed = (
        lax.all_gather(hidden, "head", axis=1, tiled=True).astype(jnp.float32) * gain[None, :]
    ).astype(jnp.bfloat16)
    projected = jnp.dot(normed, joined, preferred_element_type=jnp.float32)
    projected = projected * inv_rms[:, None]
    tok_index = lax.axis_index("seq") * tok_rows + jnp.arange(tok_rows)
    positions = tok_index.astype(jnp.float32)
    keys = rotate(projected[:, :head_size], positions).astype(jnp.bfloat16)
    vmag = jnp.mean(jnp.abs(projected[:, head_size:]), axis=1)
    window = queries.shape[0]
    group_heads = queries.shape[1] // head_size
    query_rows = queries.reshape(window * group_heads, head_size)
    scores = lax.dot_general(
        query_rows, keys, (((1,), (1,)), ((), ())), preferred_element_type=jnp.float32
    ) * head_size ** (-0.5)
    total_tokens = tok_rows * lax.axis_size("seq")
    limit = jnp.repeat(total_tokens - window + jnp.arange(window), group_heads)
    allowed = tok_index[None, :] <= limit[:, None]
    scores = jnp.where(allowed, scores, jnp.float32(-1e30))
    local_top = jnp.max(scores, axis=1)
    local_expo = jnp.exp(scores - local_top[:, None])
    local_total = jnp.sum(local_expo, axis=1)
    row_top, row_total = joined_all((local_top, local_total), "seq", combine_stats)
    rescale = jnp.exp(local_top - row_top)
    used = (jnp.arange(window) >= window - window_len[0]).astype(jnp.float32)
    row_weight = jnp.repeat(used, group_heads) * rescale / row_total
    column = jnp.dot(row_weight, local_expo, precision=lax.Precision.HIGHEST) * vmag
    reach = (KERNEL_LIMIT - 1) // 2
    padded = with_halo(column, (("seq", 0),), reach)
    kernel_halfspan = (kernel_width[0] - 1) // 2
    pooled = column
    for shift in range(1, reach + 1):
        wider = jnp.maximum(
            jnp.maximum(pooled, padded[reach + shift : reach + shift + tok_rows]),
            padded[reach - shift : reach - shift + tok_rows],
        )
        pooled = jnp.where(shift <= kernel_halfspan, wider, pooled)
    local_blocks = jnp.sum(pooled.reshape(tok_rows // BLK, BLK), axis=1)[None, :]
    everything = gathered_copies(local_blocks, "seq", 1)[0]
    ordered = -jnp.sort(-everything)
    ranks = jnp.arange(ordered.shape[0])
    kept = jnp.sum(jnp.where(ranks < kept_block_count[0], ordered, jnp.float32(0.0)))
    fraction = (kept / jnp.sum(ordered)).reshape(1)
    return (local_blocks, fraction)


def solution(mesh):
    return jax.shard_map(
        local,
        mesh=mesh,
        in_specs=(
            P("seq", "head"),
            P(),
            P(None, "head"),
            P(None, "head"),
            P(None, "head"),
            P("head"),
            P("head"),
            P("head"),
        ),
        out_specs=(P("head", "seq"), P("head")),
        check_vma=False,
    )
```

profile of v0, /device:TPU:2, one launch (start us, length us, event | category | flops | bytes accessed | tf_op | source)
XLA Modules:
  0.0 133.7 jit_solution(4325078742741071064)
XLA Ops:
  7.2 0.7 all-gather.2.cloned.1.call-update
  7.9 1.5 %multiply_reduce_fusion = f32[512]{0:T(512)S(1)} fusion(bf16[512,1024]{1,0:T(8,128)(2,1)} %param.8), kind=kLoop, calls=%fused_computation.6 | loop fusion | flops 1572352 | bytes 1050624 | tf_op jit(solution)/shard_map/reduce_sum | solution.py:100
  9.4 0.6 broadcast_in_dim.21
  10.0 5.5 %all-to-all-start = ((f32[8,1,512]{2,1,0:T(1,128)}), f32[8,1,512]{2,1,0:T(1,128)S(1)}, u32[]{:S(2)}, u32[]{:S(2)}) async-start(f32[8,1,512]{2,1,0:T(1,128)} %broadcast_in_dim.21), calls=%async_computation | async-start | bytes 32768 | tf_op jit(solution)/shard_map/all_to_all | solution.py:12
  15.5 1.0 reshape.69
  16.5 0.1 broadcast_in_dim.20
  16.6 0.1 le.16
  16.7 2.8 %all-to-all-done = f32[8,1,512]{2,1,0:T(1,128)S(1)} async-done(((f32[8,1,512]{2,1,0:T(1,128)}), f32[8,1,512]{2,1,0:T(1,128)S(1)}, u32[]{:S(2)}, u32[]{:S(2)}) %all-to-all-start) | async-done | bytes 16416 | tf_op jit(solution)/shard_map/all_to_all | solution.py:12
  19.4 44.7 %all-gather.2.cloned.1.call-done = bf16[512,8192]{1,0:T(8,128)(2,1)} async-done(((bf16[512,1024]{1,0:T(8,128)(2,1)}), bf16[512,8192]{1,0:T(8,128)(2,1)}) %all-gather.2.cloned.1.call-update) | async-done | bytes 8388624 | tf_op jit(solution)/shard_map/all_gather | solution.py:104
  64.2 7.0 %fusion.7 = f32[512,256]{0,1:T(8,128)S(1)} fusion(bf16[8192,128]{1,0:T(8,128)(2,1)} %param.11, bf16[8192,128]{1,0:T(8,128)(2,1)} %param.10, bf16[512,8192]{1,0:T(8,128)(2,1)} %all-gather.2.cloned.1.call-done, f32[8192]{0:T(1024)} %param.9, f32[512]{0:T(512)S(1)} %add_rsqrt_fusion), kind=kOutput, calls=%fused_computation.10 | convolution fusion | flops 2168586240 | bytes 13142016 | tf_op jit(solution)/shard_map/dot_general | solution.py:106
  71.2 0.6 fusion.19
  71.7 0.4 fusion.33
  72.1 0.2 fusion.11
  72.3 0.7 broadcast_in_dim.44
  73.0 9.8 %all-to-all-start.1 = ((f32[32,2,512]{2,1,0:T(2,128)}), f32[32,2,512]{2,1,0:T(2,128)S(1)}, u32[]{:S(2)}, u32[]{:S(2)}) async-start(f32[32,2,512]{2,1,0:T(2,128)} %broadcast_in_dim.44), calls=%async_computation.1 | async-start | bytes 262144 | tf_op jit(solution)/shard_map/all_to_all | solution.py:12
  84.1 0.1 broadcast_in_dim.19
  84.2 0.1 reshape.68
  84.4 9.1 %all-to-all-done.1 = f32[32,2,512]{2,1,0:T(2,128)S(1)} async-done(((f32[32,2,512]{2,1,0:T(2,128)}), f32[32,2,512]{2,1,0:T(2,128)S(1)}, u32[]{:S(2)}, u32[]{:S(2)}) %all-to-all-start.1) | async-done | bytes 131104 | tf_op jit(solution)/shard_map/all_to_all | solution.py:12
  93.5 0.1 fusion.31
  94.1 1.0 fusion.10
  95.1 0.1 fusion.32
  95.2 1.3 collective-permute-start
  96.5 4.5 %collective-permute-start.1 = (f32[7]{0:T(128)S(1)}, f32[7]{0:T(128)S(1)}, u32[]{:S(2)}, u32[]{:S(2)}) collective-permute-start(f32[7]{0:T(128)S(1)} %get-tuple-element.24), channel_id=1, source_target_pairs={{0,8},{8,16},{16,24},{24,32},{32,40},{40,48},{48,56},{56,64},{64,7... | collective-permute-start | bytes 92 | tf_op jit(solution)/shard_map/ppermute | solution.py:56
  101.1 1.3 collective-permute-done.1
  102.3 0.1 pad_maximum_fusion.1
  102.4 0.2 bitcast_reduce_fusion
  102.6 0.6 broadcast_in_dim.46
  103.2 7.8 %all-to-all-start.2 = ((f32[32,1,4]{2,1,0:T(1,128)}), f32[32,1,4]{2,1,0:T(1,128)S(1)}, u32[]{:S(2)}, u32[]{:S(2)}) async-start(f32[32,1,4]{2,1,0:T(1,128)} %broadcast_in_dim.46), calls=%async_computation.2 | async-start | bytes 32768 | tf_op jit(solution)/shard_map/all_to_all | solution.py:12
  111.7 9.2 %all-to-all-done.2 = f32[32,1,4]{2,1,0:T(1,128)S(1)} async-done(((f32[32,1,4]{2,1,0:T(1,128)}), f32[32,1,4]{2,1,0:T(1,128)S(1)}, u32[]{:S(2)}, u32[]{:S(2)}) %all-to-all-start.2) | async-done | bytes 544 | tf_op jit(solution)/shard_map/all_to_all | solution.py:12
  120.9 0.1 neg.20
  121.0 2.6 %sort.15 = (f32[128]{0:T(128)S(1)}, s32[128]{0:T(128)}) sort(f32[128]{0:T(128)S(1)} %neg.20, s32[128]{0:T(128)S(1)} %iota.29), dimensions={0}, to_apply=%region_6.7 | sort | flops 896 | bytes 2048 | tf_op jit(solution)/shard_map/jit(sort)/sort | solution.py:142
  123.6 0.7 fusion.30
  (39 shorter events, 0.7 us)
Async XLA Ops:
  7.2 57.0 %all-gather.2.cloned.1.call-start = ((), (), s32[]{:S(2)}) async-start(), calls=%async_computation.3 | async-start | bytes 9437184 | tf_op jit(solution)/shard_map/all_gather | solution.py:104
  10.0 9.4 %all-to-all-start = ((f32[8,1,512]{2,1,0:T(1,128)}), f32[8,1,512]{2,1,0:T(1,128)S(1)}, u32[]{:S(2)}, u32[]{:S(2)}) async-start(f32[8,1,512]{2,1,0:T(1,128)} %broadcast_in_dim.21), calls=%async_computation | async-start | bytes 32768 | tf_op jit(solution)/shard_map/all_to_all | solution.py:12
  73.0 20.6 %all-to-all-start.1 = ((f32[32,2,512]{2,1,0:T(2,128)}), f32[32,2,512]{2,1,0:T(2,128)S(1)}, u32[]{:S(2)}, u32[]{:S(2)}) async-start(f32[32,2,512]{2,1,0:T(2,128)} %broadcast_in_dim.44), calls=%async_computation.1 | async-start | bytes 262144 | tf_op jit(solution)/shard_map/all_to_all | solution.py:12
  95.2 5.9 %collective-permute-start = (f32[7]{0:T(128)S(1)}, f32[7]{0:T(128)S(1)}, u32[]{:S(2)}, u32[]{:S(2)}) collective-permute-start(f32[7]{0:T(128)S(1)} %get-tuple-element.23), channel_id=1, source_target_pairs={{8,0},{16,8},{24,16},{32,24},{40,32},{48,40},{56,48},{64,56},{72,6... | collective-permute-start | bytes 92 | tf_op jit(solution)/shard_map/ppermute | solution.py:57
  96.5 5.8 %collective-permute-start.1 = (f32[7]{0:T(128)S(1)}, f32[7]{0:T(128)S(1)}, u32[]{:S(2)}, u32[]{:S(2)}) collective-permute-start(f32[7]{0:T(128)S(1)} %get-tuple-element.24), channel_id=1, source_target_pairs={{0,8},{8,16},{16,24},{24,32},{32,40},{40,48},{48,56},{56,64},{64,7... | collective-permute-start | bytes 92 | tf_op jit(solution)/shard_map/ppermute | solution.py:56
  102.6 23.1 %copy-start = (f32[4]{0:T(128)}, f32[4]{0:T(128)S(1)}, u32[]{:S(2)}) copy-start(f32[4]{0:T(128)S(1)} %bitcast_reduce_fusion) | copy-start | bytes 52
  103.2 17.7 %all-to-all-start.2 = ((f32[32,1,4]{2,1,0:T(1,128)}), f32[32,1,4]{2,1,0:T(1,128)S(1)}, u32[]{:S(2)}, u32[]{:S(2)}) async-start(f32[32,1,4]{2,1,0:T(1,128)} %broadcast_in_dim.46), calls=%async_computation.2 | async-start | bytes 32768 | tf_op jit(solution)/shard_map/all_to_all | solution.py:12
Sparse Core Ops, SparseCore 0:
  9.8 54.3 all-gather.1
where the time goes:
time: 134 us
  waiting for transfers between devices  67.7 us (51%)
  starting transfers between devices  29 us (22%)
  between operations  18.7 us (14%)
  matrix products  8.29 us (6%)
  other arithmetic  6.1 us (5%)
  local copies, waits for them, and re-layouts  3.82 us (3%)
    all_gather x1, waiting for transfers between devices, local(): lax.all_gather(hidden, 'head', axis=1, tiled=True).astype(jnp.float32)  44.7 us
    all_to_all x3, starting transfers between devices, copy_for_each(): lax.all_to_all(jnp.broadcast_to(x[None], (count, *x.shape)), axis, 0, 0,...  23.1 us
    all_to_all x3, waiting for transfers between devices, copy_for_each(): lax.all_to_all(jnp.broadcast_to(x[None], (count, *x.shape)), axis, 0, 0,...  21.1 us
    dot_general x1, matrix products, local(): projected = jnp.dot(normed, joined, preferred_element_type=jnp.float32)  6.96 us
    ppermute x1, starting transfers between devices, with_halo(): before = lax.ppermute(last, axis, up)  4.55 us
  transfers between devices with their start and end apart: 6, of which 5 were waited for; matrix products, arithmetic and copies ran while one was open for 3% of the time, Pallas kernels for 0%

commit v1 on v0

--- a/solution.py
+++ b/solution.py
@@ -93,6 +93,33 @@
 def local(
     hidden, gain, key_matrix, value_matrix, queries, window_len, kernel_width, kept_block_count
 ):
+
+    def move_the_squares(arr):
+        u1 = lax.axis_size("head")
+        even = lax.axis_index("head")
+        side_arr, carry_in, w1 = (u1, even, arr.shape[1])
+        all_rows = []
+        for c in range(side_arr):
+            all_rows.append((c, (c + 1) % side_arr))
+        windows = []
+        for c in range(side_arr):
+            windows.append((c, (c - 1) % side_arr))
+        base_arr = jnp.zeros((*arr.shape[:1], side_arr * w1, *arr.shape[2:]), arr.dtype)
+        base_arr = lax.dynamic_update_slice_in_dim(base_arr, arr, carry_in * w1, axis=1)
+        found_now = field_out = arr
+        carry_out = side_arr // 2
+        for q in range(1, carry_out + 1):
+            found_now = lax.ppermute(found_now, "head", all_rows)
+            base_arr = lax.dynamic_update_slice_in_dim(
+                base_arr, found_now, (carry_in - q) % side_arr * w1, axis=1
+            )
+            if q < side_arr - carry_out:
+                field_out = lax.ppermute(field_out, "head", windows)
+                base_arr = lax.dynamic_update_slice_in_dim(
+                    base_arr, field_out, (carry_in + q) % side_arr * w1, axis=1
+                )
+        return base_arr
+
     tok_rows = hidden.shape[0]
     full_width = gain.shape[0]
     head_size = key_matrix.shape[1]
@@ -100,9 +127,7 @@
     sumsq = taken_together(jnp.sum(floats * floats, axis=1), "head")
     inv_rms = lax.rsqrt(sumsq / full_width + 1e-05)
     joined = jnp.concatenate([key_matrix, value_matrix], axis=1)
-    normed = (
-        lax.all_gather(hidden, "head", axis=1, tiled=True).astype(jnp.float32) * gain[None, :]
-    ).astype(jnp.bfloat16)
+    normed = (move_the_squares(hidden).astype(jnp.float32) * gain[None, :]).astype(jnp.bfloat16)
     projected = jnp.dot(normed, joined, preferred_element_type=jnp.float32)
     projected = projected * inv_rms[:, None]
     tok_index = lax.axis_index("seq") * tok_rows + jnp.arange(tok_rows)

time: 134 us -> 127 us (0.948); the launches traced: 134 us -> 124 us
  waiting for transfers between devices: 67.7 us -> 49.9 us
  local copies, waits for them, and re-layouts: 3.82 us -> 19.4 us
  between operations: 18.7 us -> 5.5 us
  starting transfers between devices: 29 us -> 36.4 us
    all_gather x1 -> x0, waiting for transfers between devices: 44.7 us -> none  [local(): lax.all_gather(hidden, 'head', axis=1, tiled=True).astype(jnp.float32)]
    ppermute x0 -> x7, waiting for transfers between devices: none -> 30.5 us  [the longest x4 27.8 us: move_the_squares(): found_now = lax.ppermute(found_now, 'head', all_rows)]
    dynamic_update_slice x0 -> x8, local copies, waits for them, and re-layouts: none -> 12.3 us  [the longest x4 6.82 us: move_the_squares(): lax.dynamic_update_slice_in_dim(base_arr, found_now, (carry_in - q) % sid...]
    ppermute x0 -> x7, starting transfers between devices: none -> 4.31 us  [the longest x3 3.98 us: move_the_squares(): field_out = lax.ppermute(field_out, 'head', windows)]
    broadcast_in_dim x0 -> x1, local copies, waits for them, and re-layouts: none -> 4.24 us  [move_the_squares(): jnp.zeros((*arr.shape[:1], side_arr * w1, *arr.shape[2:]), arr.dtype)]
    all_to_all x3, starting transfers between devices: 23.1 us -> 26.2 us  [copy_for_each(): lax.all_to_all(jnp.broadcast_to(x[None], (count, *x.shape)), axis, 0, 0,...]
    all_to_all x3, waiting for transfers between devices: 21.1 us -> 18.1 us  [copy_for_each(): lax.all_to_all(jnp.broadcast_to(x[None], (count, *x.shape)), axis, 0, 0,...]
  transfers between devices with their start and end apart: 6 -> 12, of which waited for: 5 -> 7; matrix products, arithmetic and copies ran while one was open for 3% -> 15% of each run, Pallas kernels for 0% -> 0%
where the time goes in v1:
time: 127 us; the launch traced here: 124 us
  waiting for transfers between devices  49.9 us (39%)
  starting transfers between devices  36.4 us (29%)
  local copies, waits for them, and re-layouts  19.4 us (15%)
  matrix products  7.14 us (6%)
  other arithmetic  6.1 us (5%)
  between operations  5.5 us (4%)
    ppermute x4, waiting for transfers between devices, move_the_squares(): found_now = lax.ppermute(found_now, 'head', all_rows)  27.8 us
    all_to_all x3, starting transfers between devices, copy_for_each(): lax.all_to_all(jnp.broadcast_to(x[None], (count, *x.shape)), axis, 0, 0,...  26.2 us
    all_to_all x3, waiting for transfers between devices, copy_for_each(): lax.all_to_all(jnp.broadcast_to(x[None], (count, *x.shape)), axis, 0, 0,...  18.1 us
    dynamic_update_slice x4, local copies, waits for them, and re-layouts, move_the_squares(): lax.dynamic_update_slice_in_dim(base_arr, found_now, (carry_in - q) % sid...  6.82 us
    dot_general x1, matrix products, local(): projected = jnp.dot(normed, joined, preferred_element_type=jnp.float32)  5.82 us
    ppermute x1, starting transfers between devices, with_halo(): before = lax.ppermute(last, axis, up)  4.55 us
    dynamic_update_slice x3, local copies, waits for them, and re-layouts, move_the_squares(): lax.dynamic_update_slice_in_dim(base_arr, field_out, (carry_in + q) % sid...  4.4 us
    broadcast_in_dim x1, local copies, waits for them, and re-layouts, move_the_squares(): jnp.zeros((*arr.shape[:1], side_arr * w1, *arr.shape[2:]), arr.dtype)  4.24 us
  transfers between devices with their start and end apart: 12, of which 7 were waited for; matrix products, arithmetic and copies ran while one was open for 15% of the time, Pallas kernels for 0%

profile of v1, /device:TPU:2, one launch (start us, length us, event | category | flops | bytes accessed | tf_op | source)
XLA Modules:
  0.0 124.4 jit_solution(11803748558204097618)
XLA Ops:
  0.7 1.7 %collective-permute-start.1 = (bf16[512,1024]{1,0:T(8,128)(2,1)}, bf16[512,1024]{1,0:T(8,128)(2,1)S(1)}, u32[]{:S(2)}, u32[]{:S(2)}) collective-permute-start(bf16[512,1024]{1,0:T(8,128)(2,1)} %param.8), channel_id=1, source_target_pairs={{0,7},{1,0},{2,1},{3,2},{4,3},{5,4},{6,5},{7,6},{8,15},{9,8},{10,9... | collective-permute-start | bytes 3145736 | tf_op jit(solution)/shard_map/ppermute | solution.py:117
  2.4 12.7 %collective-permute-done = bf16[512,1024]{1,0:T(8,128)(2,1)S(1)} collective-permute-done((bf16[512,1024]{1,0:T(8,128)(2,1)}, bf16[512,1024]{1,0:T(8,128)(2,1)S(1)}, u32[]{:S(2)}, u32[]{:S(2)}) %collective-permute-start) | collective-permute-done | bytes 1048608 | tf_op jit(solution)/shard_map/ppermute | solution.py:112
  15.1 2.0 %collective-permute-start.3 = (bf16[512,1024]{1,0:T(8,128)(2,1)S(1)}, bf16[512,1024]{1,0:T(8,128)(2,1)}, u32[]{:S(2)}, u32[]{:S(2)}) collective-permute-start(bf16[512,1024]{1,0:T(8,128)(2,1)S(1)} %collective-permute-done.1), channel_id=1, source_target_pairs={{0,7},{1,0},{2,1},{3,2},{4,3},{5,4},{6,5},{7,6},{8,15},{9,8},{10,9... | collective-permute-start | bytes 3145736 | tf_op jit(solution)/shard_map/ppermute | solution.py:117
  17.1 12.3 %collective-permute-done.2 = bf16[512,1024]{1,0:T(8,128)(2,1)} collective-permute-done((bf16[512,1024]{1,0:T(8,128)(2,1)S(1)}, bf16[512,1024]{1,0:T(8,128)(2,1)}, u32[]{:S(2)}, u32[]{:S(2)}) %collective-permute-start.2) | collective-permute-done | bytes 1048608 | tf_op jit(solution)/shard_map/ppermute | solution.py:112
  29.4 1.5 %multiply_reduce_fusion = f32[512]{0:T(512)S(1)} fusion(bf16[512,1024]{1,0:T(8,128)(2,1)} %param.8), kind=kLoop, calls=%fused_computation.6 | loop fusion | flops 1572352 | bytes 1050624 | tf_op jit(solution)/shard_map/reduce_sum | solution.py:127
  30.9 0.6 broadcast_in_dim.46
  31.5 8.9 %all-to-all-start = ((f32[8,1,512]{2,1,0:T(1,128)}), f32[8,1,512]{2,1,0:T(1,128)S(1)}, u32[]{:S(2)}, u32[]{:S(2)}) async-start(f32[8,1,512]{2,1,0:T(1,128)} %broadcast_in_dim.46), calls=%async_computation | async-start | bytes 32768 | tf_op jit(solution)/shard_map/all_to_all | solution.py:12
  40.4 4.2 %broadcast_in_dim.23 = bf16[512,8192]{1,0:T(8,128)(2,1)} broadcast(bf16[]{:T(256)} %constant.112.clone.1), dimensions={} | broadcast | bytes 8388610 | tf_op jit(solution)/shard_map/broadcast_in_dim | solution.py:107
  44.7 1.0 constant_dynamic-update-slice_fusion.7
  46.8 1.1 constant_dynamic-update-slice_fusion.6
  47.9 1.0 constant_dynamic-update-slice_fusion.5
  48.9 2.3 %constant_dynamic-update-slice_fusion.4 = bf16[512,8192]{1,0:T(8,128)(2,1)} fusion(bf16[512,8192]{1,0:T(8,128)(2,1)} %constant_dynamic-update-slice_fusion.5, bf16[512,1024]{1,0:T(8,128)(2,1)} %collective-permute-done.2, s32[]{:T(128)S(6)} %select_n.141), kind=kLoop, calls=%fused_computation.52 | loop fusion | bytes 2097156 | tf_op jit(solution)/shard_map/dynamic_update_slice | solution.py:113
  51.3 2.3 %constant_dynamic-update-slice_fusion.3 = bf16[512,8192]{1,0:T(8,128)(2,1)} fusion(bf16[512,8192]{1,0:T(8,128)(2,1)} %constant_dynamic-update-slice_fusion.4, bf16[512,1024]{1,0:T(8,128)(2,1)} %collective-permute-done.3, s32[]{:T(128)S(6)} %select_n.143), kind=kLoop, calls=%fused_computation.51 | loop fusion | bytes 2097156 | tf_op jit(solution)/shard_map/dynamic_update_slice | solution.py:118
  53.6 2.3 %constant_dynamic-update-slice_fusion.2 = bf16[512,8192]{1,0:T(8,128)(2,1)} fusion(bf16[512,8192]{1,0:T(8,128)(2,1)} %constant_dynamic-update-slice_fusion.3, bf16[512,1024]{1,0:T(8,128)(2,1)} %collective-permute-done.4, s32[]{:T(128)S(6)} %select_n.145), kind=kLoop, calls=%fused_computation.50 | loop fusion | bytes 2097156 | tf_op jit(solution)/shard_map/dynamic_update_slice | solution.py:113
  55.8 2.7 %collective-permute-done.5 = bf16[512,1024]{1,0:T(8,128)(2,1)S(1)} collective-permute-done((bf16[512,1024]{1,0:T(8,128)(2,1)}, bf16[512,1024]{1,0:T(8,128)(2,1)S(1)}, u32[]{:S(2)}, u32[]{:S(2)}) %collective-permute-start.5) | collective-permute-done | bytes 1048608 | tf_op jit(solution)/shard_map/ppermute | solution.py:117
  58.6 1.1 constant_dynamic-update-slice_fusion.1
  59.6 2.8 %collective-permute-done.6 = bf16[512,1024]{1,0:T(8,128)(2,1)S(1)} collective-permute-done((bf16[512,1024]{1,0:T(8,128)(2,1)}, bf16[512,1024]{1,0:T(8,128)(2,1)S(1)}, u32[]{:S(2)}, u32[]{:S(2)}) %collective-permute-start.6) | collective-permute-done | bytes 1048608 | tf_op jit(solution)/shard_map/ppermute | solution.py:112
  62.5 1.1 constant_dynamic-update-slice_fusion
  63.5 5.8 %fusion.7 = f32[512,256]{0,1:T(8,128)S(1)} fusion(bf16[8192,128]{1,0:T(8,128)(2,1)S(1)} %copy-done.3, bf16[8192,128]{1,0:T(8,128)(2,1)S(1)} %copy-done.4, bf16[512,8192]{1,0:T(8,128)(2,1)} %constant_dynamic-update-slice_fusion, f32[8192]{0:T(1024)S(1)} %copy-done.5, f32[512]{0:T(512)S(1)} %add_rsqrt_fusion), kind=kOutput, calls=%fused_computation.10 | convolution fusion | flops 2168586240 | bytes 13142016 | tf_op jit(solution)/shard_map/dot_general | solution.py:131
  69.4 0.6 fusion.19
  70.5 0.7 broadcast_in_dim.48
  71.2 9.8 %all-to-all-start.1 = ((f32[32,2,512]{2,1,0:T(2,128)}), f32[32,2,512]{2,1,0:T(2,128)S(1)}, u32[]{:S(2)}, u32[]{:S(2)}) async-start(f32[32,2,512]{2,1,0:T(2,128)} %broadcast_in_dim.48), calls=%async_computation.1 | async-start | bytes 262144 | tf_op jit(solution)/shard_map/all_to_all | solution.py:12
  82.5 8.9 %all-to-all-done.1 = f32[32,2,512]{2,1,0:T(2,128)S(1)} async-done(((f32[32,2,512]{2,1,0:T(2,128)}), f32[32,2,512]{2,1,0:T(2,128)S(1)}, u32[]{:S(2)}, u32[]{:S(2)}) %all-to-all-start.1) | async-done | bytes 131104 | tf_op jit(solution)/shard_map/all_to_all | solution.py:12
  92.0 1.0 fusion.10
  93.1 1.3 %collective-permute-start.7 = (f32[7]{0:T(128)S(1)}, f32[7]{0:T(128)S(1)}, u32[]{:S(2)}, u32[]{:S(2)}) collective-permute-start(f32[7]{0:T(128)S(1)} %get-tuple-element.23), channel_id=1, source_target_pairs={{8,0},{16,8},{24,16},{32,24},{40,32},{48,40},{56,48},{64,56},{72,6... | collective-permute-start | bytes 92 | tf_op jit(solution)/shard_map/ppermute | solution.py:57
  94.4 4.5 %collective-permute-start.8 = (f32[7]{0:T(128)S(1)}, f32[7]{0:T(128)S(1)}, u32[]{:S(2)}, u32[]{:S(2)}) collective-permute-start(f32[7]{0:T(128)S(1)} %get-tuple-element.24), channel_id=1, source_target_pairs={{0,8},{8,16},{16,24},{24,32},{32,40},{40,48},{48,56},{56,64},{64,7... | collective-permute-start | bytes 92 | tf_op jit(solution)/shard_map/ppermute | solution.py:56
  98.9 1.3 %collective-permute-done.8 = f32[7]{0:T(128)S(1)} collective-permute-done((f32[7]{0:T(128)S(1)}, f32[7]{0:T(128)S(1)}, u32[]{:S(2)}, u32[]{:S(2)}) %collective-permute-start.8) | collective-permute-done | bytes 60 | tf_op jit(solution)/shard_map/ppermute | solution.py:56
  100.5 0.6 broadcast_in_dim.50
  101.1 7.5 %all-to-all-start.2 = ((f32[32,1,4]{2,1,0:T(1,128)}), f32[32,1,4]{2,1,0:T(1,128)S(1)}, u32[]{:S(2)}, u32[]{:S(2)}) async-start(f32[32,1,4]{2,1,0:T(1,128)} %broadcast_in_dim.50), calls=%async_computation.2 | async-start | bytes 32768 | tf_op jit(solution)/shard_map/all_to_all | solution.py:12
  109.3 9.2 %all-to-all-done.2 = f32[32,1,4]{2,1,0:T(1,128)S(1)} async-done(((f32[32,1,4]{2,1,0:T(1,128)}), f32[32,1,4]{2,1,0:T(1,128)S(1)}, u32[]{:S(2)}, u32[]{:S(2)}) %all-to-all-start.2) | async-done | bytes 544 | tf_op jit(solution)/shard_map/all_to_all | solution.py:12
  118.6 2.6 %sort.15 = (f32[128]{0:T(128)S(1)}, s32[128]{0:T(128)}) sort(f32[128]{0:T(128)S(1)} %neg.20, s32[128]{0:T(128)S(1)} %iota.29), dimensions={0}, to_apply=%region_6.7 | sort | flops 896 | bytes 2048 | tf_op jit(solution)/shard_map/jit(sort)/sort | solution.py:167
  121.2 0.7 fusion.30
  (69 shorter events, 2.7 us)
Async XLA Ops:
  0.6 44.1 %copy-start = (bf16[512,1024]{1,0:T(8,128)(2,1)S(1)}, bf16[512,1024]{1,0:T(8,128)(2,1)}, u32[]{:S(2)}) copy-start(bf16[512,1024]{1,0:T(8,128)(2,1)} %param.8) | copy-start | bytes 3145732
  0.6 45.4 %copy-start.1 = (bf16[64,1024]{1,0:T(8,128)(2,1)S(1)}, bf16[64,1024]{1,0:T(8,128)(2,1)}, u32[]{:S(2)}) copy-start(bf16[64,1024]{1,0:T(8,128)(2,1)} %param.12) | copy-start | bytes 393220
  0.6 14.4 %collective-permute-start = (bf16[512,1024]{1,0:T(8,128)(2,1)}, bf16[512,1024]{1,0:T(8,128)(2,1)S(1)}, u32[]{:S(2)}, u32[]{:S(2)}) collective-permute-start(bf16[512,1024]{1,0:T(8,128)(2,1)} %param.8), channel_id=1, source_target_pairs={{0,1},{1,2},{2,3},{3,4},{4,5},{5,6},{6,7},{7,0},{8,9},{9,10},{10,1... | collective-permute-start | bytes 3145736 | tf_op jit(solution)/shard_map/ppermute | solution.py:112
  0.7 14.4 %collective-permute-start.1 = (bf16[512,1024]{1,0:T(8,128)(2,1)}, bf16[512,1024]{1,0:T(8,128)(2,1)S(1)}, u32[]{:S(2)}, u32[]{:S(2)}) collective-permute-start(bf16[512,1024]{1,0:T(8,128)(2,1)} %param.8), channel_id=1, source_target_pairs={{0,7},{1,0},{2,1},{3,2},{4,3},{5,4},{6,5},{7,6},{8,15},{9,8},{10,9... | collective-permute-start | bytes 3145736 | tf_op jit(solution)/shard_map/ppermute | solution.py:117
  15.1 14.3 %collective-permute-start.2 = (bf16[512,1024]{1,0:T(8,128)(2,1)S(1)}, bf16[512,1024]{1,0:T(8,128)(2,1)}, u32[]{:S(2)}, u32[]{:S(2)}) collective-permute-start(bf16[512,1024]{1,0:T(8,128)(2,1)S(1)} %collective-permute-done), channel_id=1, source_target_pairs={{0,1},{1,2},{2,3},{3,4},{4,5},{5,6},{6,7},{7,0},{8,9},{9,10},{10,1... | collective-permute-start | bytes 3145736 | tf_op jit(solution)/shard_map/ppermute | solution.py:112
  15.1 30.6 %collective-permute-start.3 = (bf16[512,1024]{1,0:T(8,128)(2,1)S(1)}, bf16[512,1024]{1,0:T(8,128)(2,1)}, u32[]{:S(2)}, u32[]{:S(2)}) collective-permute-start(bf16[512,1024]{1,0:T(8,128)(2,1)S(1)} %collective-permute-done.1), channel_id=1, source_target_pairs={{0,7},{1,0},{2,1},{3,2},{4,3},{5,4},{6,5},{7,6},{8,15},{9,8},{10,9... | collective-permute-start | bytes 3145736 | tf_op jit(solution)/shard_map/ppermute | solution.py:117
  29.4 17.0 %collective-permute-start.4 = (bf16[512,1024]{1,0:T(8,128)(2,1)}, bf16[512,1024]{1,0:T(8,128)(2,1)}, u32[]{:S(2)}, u32[]{:S(2)}) collective-permute-start(bf16[512,1024]{1,0:T(8,128)(2,1)} %collective-permute-done.2), channel_id=1, source_target_pairs={{0,1},{1,2},{2,3},{3,4},{4,5},{5,6},{6,7},{7,0},{8,9},{9,10},{10,1... | collective-permute-start | bytes 3145736 | tf_op jit(solution)/shard_map/ppermute | solution.py:112
  31.5 14.8 %all-to-all-start = ((f32[8,1,512]{2,1,0:T(1,128)}), f32[8,1,512]{2,1,0:T(1,128)S(1)}, u32[]{:S(2)}, u32[]{:S(2)}) async-start(f32[8,1,512]{2,1,0:T(1,128)} %broadcast_in_dim.46), calls=%async_computation | async-start | bytes 32768 | tf_op jit(solution)/shard_map/all_to_all | solution.py:12
  44.7 18.8 %copy-start.5 = (f32[8192]{0:T(1024)S(1)}, f32[8192]{0:T(1024)}, u32[]{:S(2)}) copy-start(f32[8192]{0:T(1024)} %param.9) | copy-start | bytes 98308
  45.7 12.8 %collective-permute-start.5 = (bf16[512,1024]{1,0:T(8,128)(2,1)}, bf16[512,1024]{1,0:T(8,128)(2,1)S(1)}, u32[]{:S(2)}, u32[]{:S(2)}) collective-permute-start(bf16[512,1024]{1,0:T(8,128)(2,1)} %collective-permute-done.3), channel_id=1, source_target_pairs={{0,7},{1,0},{2,1},{3,2},{4,3},{5,4},{6,5},{7,6},{8,15},{9,8},{10,9... | collective-permute-start | bytes 3145736 | tf_op jit(solution)/shard_map/ppermute | solution.py:117
  46.4 17.1 %copy-start.3 = (bf16[8192,128]{1,0:T(8,128)(2,1)S(1)}, bf16[8192,128]{1,0:T(8,128)(2,1)}, u32[]{:S(2)}) copy-start(bf16[8192,128]{1,0:T(8,128)(2,1)} %param.11) | copy-start | bytes 6291460
  46.4 17.1 %copy-start.4 = (bf16[8192,128]{1,0:T(8,128)(2,1)S(1)}, bf16[8192,128]{1,0:T(8,128)(2,1)}, u32[]{:S(2)}) copy-start(bf16[8192,128]{1,0:T(8,128)(2,1)} %param.10) | copy-start | bytes 6291460
  46.4 16.0 %collective-permute-start.6 = (bf16[512,1024]{1,0:T(8,128)(2,1)}, bf16[512,1024]{1,0:T(8,128)(2,1)S(1)}, u32[]{:S(2)}, u32[]{:S(2)}) collective-permute-start(bf16[512,1024]{1,0:T(8,128)(2,1)} %collective-permute-done.4), channel_id=1, source_target_pairs={{0,1},{1,2},{2,3},{3,4},{4,5},{5,6},{6,7},{7,0},{8,9},{9,10},{10,1... | collective-permute-start | bytes 3145736 | tf_op jit(solution)/shard_map/ppermute | solution.py:112
  71.2 20.2 %all-to-all-start.1 = ((f32[32,2,512]{2,1,0:T(2,128)}), f32[32,2,512]{2,1,0:T(2,128)S(1)}, u32[]{:S(2)}, u32[]{:S(2)}) async-start(f32[32,2,512]{2,1,0:T(2,128)} %broadcast_in_dim.48), calls=%async_computation.1 | async-start | bytes 262144 | tf_op jit(solution)/shard_map/all_to_all | solution.py:12
  93.1 5.9 %collective-permute-start.7 = (f32[7]{0:T(128)S(1)}, f32[7]{0:T(128)S(1)}, u32[]{:S(2)}, u32[]{:S(2)}) collective-permute-start(f32[7]{0:T(128)S(1)} %get-tuple-element.23), channel_id=1, source_target_pairs={{8,0},{16,8},{24,16},{32,24},{40,32},{48,40},{56,48},{64,56},{72,6... | collective-permute-start | bytes 92 | tf_op jit(solution)/shard_map/ppermute | solution.py:57
  94.4 5.8 %collective-permute-start.8 = (f32[7]{0:T(128)S(1)}, f32[7]{0:T(128)S(1)}, u32[]{:S(2)}, u32[]{:S(2)}) collective-permute-start(f32[7]{0:T(128)S(1)} %get-tuple-element.24), channel_id=1, source_target_pairs={{0,8},{8,16},{16,24},{24,32},{32,40},{40,48},{48,56},{56,64},{64,7... | collective-permute-start | bytes 92 | tf_op jit(solution)/shard_map/ppermute | solution.py:56
  100.5 22.8 %copy-start.2 = (f32[4]{0:T(128)}, f32[4]{0:T(128)S(1)}, u32[]{:S(2)}) copy-start(f32[4]{0:T(128)S(1)} %bitcast_reduce_fusion) | copy-start | bytes 52
  101.1 17.3 %all-to-all-start.2 = ((f32[32,1,4]{2,1,0:T(1,128)}), f32[32,1,4]{2,1,0:T(1,128)S(1)}, u32[]{:S(2)}, u32[]{:S(2)}) async-start(f32[32,1,4]{2,1,0:T(1,128)} %broadcast_in_dim.50), calls=%async_computation.2 | async-start | bytes 32768 | tf_op jit(solution)/shard_map/all_to_all | solution.py:12
